TPU v7x, 512 devices: a whole 4x8x8 slice. The times are simulated.
512 devices in a mesh: seq: 32 (over y, x), head: 16 (over z, core).
Axes of the slice: x: 4, y: 8, z: 8, core: 2. Of those that a mesh axis runs over, the one named last changes fastest.
Arguments:
- queries: bfloat16 [65536, 2048], P('seq', 'head'), may hold values from -4.5 to 4.5
- key_vectors: bfloat16 [65536, 2048], P('seq', 'head'), may hold values from -4.5 to 4.5
- value_vectors: bfloat16 [65536, 2048], P('seq', 'head'), may hold values from -18 to 18
- w_out: bfloat16 [2048, 2048], P('seq'), may hold values from -0.125 to 0.125
Outputs:
- projected: bfloat16 [65536, 2048], P(('seq', 'head'))
All inputs are finite; a program needn't handle non-finite values.
Results may differ from a plain program's by a relative error of at most 0.0053.
Values may be sent and summed in bfloat16 or wider, within the bound.
No kernel may reach another device: no remote copies, remote signals or barrier semaphores. Data moves between devices by JAX's collectives and lax.ppermute only.
A program may use at most 64 MiB of HBM per device.

v0:
```python
import math
import jax
import jax.numpy as jnp
from jax import lax
from jax.sharding import PartitionSpec as P

HD = 128
W = 1024
norm_eps = 1e-06


def passed_along(shard, axis, by):
    count = lax.axis_size(axis)
    pairs = [(i, i + by) for i in range(count) if 0 <= i + by < count]
    return lax.ppermute(shard, axis, pairs)


def carried_in(part, axis, combine, identity):
    place = lax.axis_index(axis)
    gathered = lax.all_gather(part, axis)
    state = jnp.zeros_like(part) + jnp.asarray(identity, part.dtype)

    def one(lap, state):
        return combine(state, lax.dynamic_index_in_dim(gathered, lap, 0, False))

    return lax.fori_loop(0, place, one, state)


def normalize(branch):
    return branch * lax.rsqrt(jnp.mean(branch * branch, axis=-1, keepdims=True) + norm_eps)


def add_states(earlier, later):
    return earlier + later


def split_pair(values):
    upper = lax.optimization_barrier(values.astype(jnp.bfloat16))
    lower = (values - upper.astype(jnp.float32)).astype(jnp.bfloat16)
    return (upper, lower)


def window_branch(query_heads, window_keys, window_values, offset):
    tok_rows, heads_here, head_width = query_heads.shape
    block_rows = min(512, tok_rows)
    key_span = block_rows + W
    score_scale = 1.0 / math.sqrt(head_width)

    def one_block(block_start):
        query_block = lax.dynamic_slice_in_dim(query_heads, block_start, block_rows, 0)
        key_block = lax.dynamic_slice_in_dim(window_keys, block_start, key_span, 0)
        value_block = lax.dynamic_slice_in_dim(window_values, block_start, key_span, 0)
        scores = (
            jnp.einsum("qhd,khd->hqk", query_block, key_block, preferred_element_type=jnp.float32)
            * score_scale
        )
        row_index = block_start + jnp.arange(block_rows, dtype=jnp.int32)[:, None]
        col_index = block_start + jnp.arange(key_span, dtype=jnp.int32)[None, :]
        allowed = (
            (col_index > row_index) & (col_index <= row_index + W) & (col_index - W + offset >= 0)
        )
        scores = jnp.where(allowed[None], scores, -jnp.inf)
        row_top = jnp.max(scores, axis=-1, keepdims=True)
        weights = jnp.where(allowed[None], jnp.exp(scores - row_top), 0.0).astype(jnp.bfloat16)
        return jnp.einsum("hqk,khd->qhd", weights, value_block, preferred_element_type=jnp.float32)

    starts = jnp.arange(tok_rows // block_rows, dtype=jnp.int32) * block_rows
    return lax.map(one_block, starts).reshape(tok_rows, heads_here, head_width)


def on_device(queries, key_vectors, value_vectors, w_out):
    tok_rows = queries.shape[0]
    heads_here = queries.shape[1] // HD
    head_shape = (tok_rows, heads_here, HD)
    query_heads = queries.reshape(head_shape)
    key_heads = key_vectors.reshape(head_shape)
    value_heads = value_vectors.reshape(head_shape)
    window_rim = jnp.stack([key_heads[tok_rows - W :], value_heads[tok_rows - W :]])
    earlier = passed_along(window_rim, "seq", 1)
    window_keys = jnp.concatenate([earlier[0], key_heads], axis=0)
    window_values = jnp.concatenate([earlier[1], value_heads], axis=0)
    offset = lax.axis_index("seq") * tok_rows
    soft_heads = window_branch(query_heads, window_keys, window_values, offset)
    block_rows = min(512, tok_rows)
    block_count = tok_rows // block_rows
    block_shape = (block_count, block_rows, heads_here, HD)
    blocked_queries = query_heads.reshape(block_shape)
    blocked_keys = key_heads.reshape(block_shape)
    blocked_values = value_heads.reshape(block_shape)
    state_increments = jnp.einsum(
        "bkhd,bkhe->bhde", blocked_keys, blocked_values, preferred_element_type=jnp.float32
    )
    own_total = jnp.sum(state_increments, axis=0)
    prior_state = carried_in(own_total, "seq", add_states, jnp.zeros_like(own_total))
    running = jnp.cumsum(state_increments, axis=0)
    preceding_state = prior_state[None] + jnp.concatenate(
        [jnp.zeros_like(state_increments[:1]), running[:-1]], axis=0
    )
    intra_block_scores = jnp.einsum(
        "bqhd,bkhd->bhqk", blocked_queries, blocked_keys, preferred_element_type=jnp.float32
    )
    causal = (
        jnp.arange(block_rows, dtype=jnp.int32)[:, None]
        >= jnp.arange(block_rows, dtype=jnp.int32)[None, :]
    )
    intra_block_scores = jnp.where(causal, intra_block_scores, 0.0)
    score_upper, score_lower = split_pair(intra_block_scores)
    local_block_terms = jnp.einsum(
        "bhqk,bkhd->bqhd", score_upper, blocked_values, preferred_element_type=jnp.float32
    )
    local_block_terms = local_block_terms + jnp.einsum(
        "bhqk,bkhd->bqhd", score_lower, blocked_values, preferred_element_type=jnp.float32
    )
    state_upper, state_lower = split_pair(preceding_state)
    carried_state_sum = jnp.einsum(
        "bqhd,bhde->bqhe", blocked_queries, state_upper, preferred_element_type=jnp.float32
    )
    carried_state_sum = carried_state_sum + jnp.einsum(
        "bqhd,bhde->bqhe", blocked_queries, state_lower, preferred_element_type=jnp.float32
    )
    linear = (local_block_terms + carried_state_sum).reshape(head_shape)
    mixed_heads = (0.5 * (normalize(soft_heads) + normalize(linear))).astype(jnp.bfloat16)
    mixed_heads = mixed_heads.reshape(tok_rows, heads_here * HD)
    regrouped = lax.all_to_all(mixed_heads, "head", split_axis=0, concat_axis=1, tiled=True)
    projected = jnp.dot(
        regrouped,
        lax.all_gather(w_out, "seq", axis=0, tiled=True),
        preferred_element_type=jnp.float32,
    )
    return projected.astype(jnp.bfloat16)


def solution(mesh):
    placed = (P("seq", "head"), P("seq", "head"), P("seq", "head"), P("seq", None))
    return jax.shard_map(
        on_device, mesh=mesh, in_specs=placed, out_specs=P(("seq", "head"), None), check_vma=False
    )
```

profile of v0, /device:TPU:1, one launch (start us, length us, event | category | flops | bytes accessed | tf_op | source)
XLA Modules:
  0.0 214.6 jit_solution(4155699273040618494)
XLA Ops:
  6.5 2.3 %fusion.41 = (f32[128,128]{1,0:T(8,128)}, f32[4,128,128]{2,1,0:T(8,128)S(1)}) fusion(bf16[4,512,128]{2,1,0:T(8,128)(2,1)} %bitcast.109, bf16[4,512,128]{2,1,0:T(8,128)(2,1)} %bitcast.105), kind=kOutput, calls=%fused_computation.63 | convolution fusion | flops 67158016 | bytes 1376256 | tf_op jit(solution)/shard_map/bkhd,bkhe->bhde/dot_general | solution.py:90
  8.9 0.7 all-gather.4.cloned.1.call-update
  9.6 1.1 slice_bitcast_fusion.2
  10.6 0.8 pad_maximum_fusion.2
  11.5 4.7 %collective-permute-start = (bf16[2,1024,1,128]{3,1,2,0:T(8,128)(2,1)}, bf16[2,1024,1,128]{3,1,2,0:T(8,128)(2,1)}, u32[]{:S(2)}, u32[]{:S(2)}) collective-permute-start(bf16[2,1024,1,128]{3,1,2,0:T(8,128)(2,1)} %pad_maximum_fusion.2), channel_id=1, source_target_pairs={{0,16},{16,32},{32,48},{48,64},{64,80},{80,96},{96,112},{112,128},... | collective-permute-start | bytes 1572872 | tf_op jit(solution)/shard_map/ppermute | solution.py:15
  16.3 0.7 fusion.42
  17.1 0.6 fusion.14
  17.7 0.4 copy-done
  18.1 1.8 fusion.16
  19.9 0.7 fusion.30
  20.6 0.9 slice.24
  21.6 2.9 %fusion.26 = f32[4,128,512]{1,2,0:T(8,128)} fusion(f32[4,512,128]{2,1,0:T(8,128)} %fusion.16, bf16[4,512,128]{2,1,0:T(8,128)(2,1)S(1)} %bitcast.107, bf16[4,1,512,512]{3,2,0,1:T(8,128)(2,1)S(1)} %fusion.14), kind=kOutput, calls=%fused_computation.35 | convolution fusion | flops 268697600 | bytes 4718592 | tf_op jit(solution)/shard_map/bhqk,bkhd->bqhd/dot_general | solution.py:108
  24.5 1.1 slice_bitcast_fusion
  25.8 36.6 %while.22 = (s32[]{:T(128)}, f32[4,512,1,128]{1,3,2,0:T(8,128)}, s32[4]{0:T(128)S(1)}, bf16[3072,1,128]{2,0,1:T(8,128)(2,1)S(1)}, s32[]{:T(128)}, /*index=5*/bf1...) while((s32[]{:T(128)}, f32[4,512,1,128]{1,3,2,0:T(8,128)}, ...), condition=%wide.region_2.3_spmd, body=%wide.region_0.2_spmd.sunk | while | flops 413671424 | bytes 7516368 | solution.py:68
  25.8 0.6 dynamic_slice.54
  29.6 0.6 iota_add_fusion.4
  30.2 0.7 add_compare_fusion.2
  30.9 0.7 iota_add_fusion.5
  31.6 1.2 fusion.57
  32.8 2.1 fusion.58
  34.9 0.6 dynamic_slice.54
  38.7 0.6 iota_add_fusion.4
  39.4 0.7 add_compare_fusion.2
  40.1 0.7 iota_add_fusion.5
  40.7 1.2 fusion.57
  41.9 2.1 fusion.58
  44.1 0.6 dynamic_slice.54
  47.9 0.6 iota_add_fusion.4
  48.5 0.7 add_compare_fusion.2
  49.2 0.7 iota_add_fusion.5
  49.9 1.2 fusion.57
  51.1 2.2 %fusion.58 = f32[4,512,1,128]{1,3,2,0:T(8,128)} fusion(f32[4,512,1,128]{1,3,2,0:T(8,128)} %get-tuple-element.263, s32[]{:T(128)} %get-tuple-element.262, f32[512,1536]{1,0:T(8,128)S(1)} %get-tuple-element.224, f32[512]{0:T(512)S(1)} %get-tuple-element.225, s32[1536]{0:T(1024)S(1)} %iota_add_fusion.5, s32[512]{0:T(512)S(1)} %get-tuple-element.222, ...), kind=kOutput, calls=%fused_computation.6.clone.1 | convolution fusion | flops 206831616 | bytes 3817988 | tf_op jit(solution)/shard_map/while/body/eval_jaxpr/hqk,khd->qhd/dot_general | solution.py:65
  53.2 0.6 dynamic_slice.54
  57.0 0.6 iota_add_fusion.4
  57.7 0.7 add_compare_fusion.2
  58.4 0.7 iota_add_fusion.5
  59.0 1.2 fusion.57
  60.2 2.2 %fusion.58 = f32[4,512,1,128]{1,3,2,0:T(8,128)} fusion(f32[4,512,1,128]{1,3,2,0:T(8,128)} %get-tuple-element.263, s32[]{:T(128)} %get-tuple-element.262, f32[512,1536]{1,0:T(8,128)S(1)} %get-tuple-element.224, f32[512]{0:T(512)S(1)} %get-tuple-element.225, s32[1536]{0:T(1024)S(1)} %iota_add_fusion.5, s32[512]{0:T(512)S(1)} %get-tuple-element.222, ...), kind=kOutput, calls=%fused_computation.6.clone.1 | convolution fusion | flops 206831616 | bytes 3817988 | tf_op jit(solution)/shard_map/while/body/eval_jaxpr/hqk,khd->qhd/dot_general | solution.py:65
  62.4 1.5 copy.11
  63.9 1.4 multiply_reduce_fusion
  65.3 29.2 %all-gather.6.cloned.1.call-done = f32[4096,128]{1,0:T(8,128)} async-done(((f32[128,128]{1,0:T(8,128)}), f32[4096,128]{1,0:T(8,128)}) %all-gather.6.cloned.1.call-update) | async-done | bytes 2097168 | tf_op jit(solution)/shard_map/all_gather | solution.py:20
  94.5 0.3 fusion.35
  94.8 1.7 fusion.29
  96.6 0.7 multiply_convert_fusion
  97.3 29.8 %all_to_all.16 = bf16[16,128,128]{2,1,0:T(8,128)(2,1)S(1)} all-to-all(bf16[16,128,128]{2,1,0:T(8,128)(2,1)S(1)} %multiply_convert_fusion), channel_id=1, replica_groups=mesh['seq'=32,'head'=16] {'head'}, dimensions={0} | all-to-all | bytes 1048576 | tf_op jit(solution)/shard_map/all_to_all | solution.py:124
  127.2 0.3 copy.17
  127.4 74.9 %all-gather.4.cloned.1.call-done = bf16[2048,2048]{1,0:T(8,128)(2,1)} async-done(((bf16[64,2048]{1,0:T(8,128)(2,1)}), bf16[2048,2048]{1,0:T(8,128)(2,1)}) %all-gather.4.cloned.1.call-update) | async-done | bytes 8388624 | tf_op jit(solution)/shard_map/all_gather | solution.py:127
  202.3 5.5 %convolution_convert_fusion = bf16[128,2048]{1,0:T(8,128)(2,1)} fusion(bf16[128,2048]{0,1:T(8,128)(2,1)S(1)} %bitcast.116, bf16[2048,2048]{1,0:T(8,128)(2,1)} %all-gather.4.cloned.1.call-done), kind=kOutput, calls=%fused_computation.24 | convolution fusion | flops 1074003968 | bytes 9437184 | tf_op jit(solution)/shard_map/dot_general | solution.py:125
  (23 shorter events, 0.3 us)
Async XLA Ops:
  6.5 9.8 %copy-start.1 = (bf16[2048,128]{1,0:T(8,128)(2,1)S(1)}, bf16[2048,128]{1,0:T(8,128)(2,1)}, u32[]{:S(2)}) copy-start(bf16[2048,128]{1,0:T(8,128)(2,1)} %param.9) | copy-start | bytes 1572868
  6.5 9.8 %copy-start.2 = (bf16[2048,128]{1,0:T(8,128)(2,1)S(1)}, bf16[2048,128]{1,0:T(8,128)(2,1)}, u32[]{:S(2)}) copy-start(bf16[2048,128]{1,0:T(8,128)(2,1)} %param.8) | copy-start | bytes 1572868
  6.5 88.0 %all-gather.6.cloned.1.call-start = ((), (), s32[]{:S(2)}) async-start(), calls=%async_computation.2 | async-start | bytes 2162688 | tf_op jit(solution)/shard_map/all_gather | solution.py:20
  8.8 193.5 %all-gather.4.cloned.1.call-start = ((), (), s32[]{:S(2)}) async-start(), calls=%async_computation.1 | async-start | bytes 8650752 | tf_op jit(solution)/shard_map/all_gather | solution.py:127
  11.5 13.0 %collective-permute-start = (bf16[2,1024,1,128]{3,1,2,0:T(8,128)(2,1)}, bf16[2,1024,1,128]{3,1,2,0:T(8,128)(2,1)}, u32[]{:S(2)}, u32[]{:S(2)}) collective-permute-start(bf16[2,1024,1,128]{3,1,2,0:T(8,128)(2,1)} %pad_maximum_fusion.2), channel_id=1, source_target_pairs={{0,16},{16,32},{32,48},{48,64},{64,80},{80,96},{96,112},{112,128},... | collective-permute-start | bytes 1572872 | tf_op jit(solution)/shard_map/ppermute | solution.py:15
  17.0 1.0 copy-start
  24.5 1.3 copy-start.3
Sparse Core Ops, SparseCore 0:
  10.5 83.9 all-gather.5
  97.7 104.5 all-gather.3
where the time goes:
time: 217 us; the launch traced here: 215 us
  waiting for transfers between devices  105 us (48%)
  blocking collectives  29.8 us (14%)
  matrix products  28.6 us (13%)
  between operations  13.5 us (6%)
  loops' own time  13 us (6%)
  other arithmetic  12.3 us (6%)
  local copies, waits for them, and re-layouts  7.72 us (4%)
  starting transfers between devices  4.79 us (2%)
    all_gather x1, waiting for transfers between devices, on_device(): lax.all_gather(w_out, 'seq', axis=0, tiled=True)  74.9 us
    all_to_all x1, blocking collectives, on_device(): lax.all_to_all(mixed_heads, 'head', split_axis=0, concat_axis=1, tiled=True)  29.8 us
    all_gather x1, waiting for transfers between devices, carried_in(): gathered = lax.all_gather(part, axis)  29.2 us
    another operation x1, loops' own time, window_branch(): return lax.map(one_block, starts).reshape(tok_rows, heads_here, head_width)  13 us
    dot_general x4, matrix products, one_block(): jnp.einsum('hqk,khd->qhd', weights, value_block, preferred_element_type=j...  8.59 us
    dot_general x1, matrix products, on_device(): jnp.dot(regrouped, lax.all_gather(w_out, 'seq', axis=0, tiled=True), pref...  5.45 us
    dot_general x4, matrix products, one_block(): jnp.einsum('qhd,khd->hqk', query_block, key_block, preferred_element_type...  4.85 us
    ppermute x1, starting transfers between devices, passed_along(): return lax.ppermute(shard, axis, pairs)  4.74 us
  transfers between devices with their start and end apart: 3, of which 2 were waited for; matrix products, arithmetic and copies ran while one was open for 19% of the time, Pallas kernels for 0%

commit v1 on v0

--- a/solution.py
+++ b/solution.py
@@ -7,6 +7,13 @@
 HD = 128
 W = 1024
 norm_eps = 1e-06
+
+
+def gather_over(shard, axis, d):
+    size = lax.axis_size(axis)
+    tiles = jnp.stack([shard for _ in range(size)])
+    tiles = lax.all_to_all(tiles, axis, split_axis=0, concat_axis=0)
+    return jnp.concatenate(tiles, axis=d)
 
 
 def passed_along(shard, axis, by):
@@ -122,11 +129,7 @@
     mixed_heads = (0.5 * (normalize(soft_heads) + normalize(linear))).astype(jnp.bfloat16)
     mixed_heads = mixed_heads.reshape(tok_rows, heads_here * HD)
     regrouped = lax.all_to_all(mixed_heads, "head", split_axis=0, concat_axis=1, tiled=True)
-    projected = jnp.dot(
-        regrouped,
-        lax.all_gather(w_out, "seq", axis=0, tiled=True),
-        preferred_element_type=jnp.float32,
-    )
+    projected = jnp.dot(regrouped, gather_over(w_out, "seq", 0), preferred_element_type=jnp.float32)
     return projected.astype(jnp.bfloat16)
 
 

time: 217 us -> 374 us (1.72)
  the two profiles are of different devices: /device:TPU:1 before, /device:TPU:31 now
where the time goes in v1:
time: 374 us; the launch traced here: 372 us
  waiting for transfers between devices  224 us (60%)
  blocking collectives  30.1 us (8%)
  matrix products  28.6 us (8%)
  other arithmetic  26.4 us (7%)
  starting transfers between devices  23.8 us (6%)
  between operations  13.6 us (4%)
  loops' own time  13.4 us (4%)
  local copies, waits for them, and re-layouts  12 us (3%)
    all_to_all x1, waiting for transfers between devices, gather_over(): tiles = lax.all_to_all(tiles, axis, split_axis=0, concat_axis=0)  198 us
    all_to_all x1, blocking collectives, on_device(): lax.all_to_all(mixed_heads, 'head', split_axis=0, concat_axis=1, tiled=True)  30.1 us
    all_gather x1, waiting for transfers between devices, carried_in(): gathered = lax.all_gather(part, axis)  23.3 us
    all_to_all x1, starting transfers between devices, gather_over(): tiles = lax.all_to_all(tiles, axis, split_axis=0, concat_axis=0)  19.5 us
    another operation x1, loops' own time, window_branch(): return lax.map(one_block, starts).reshape(tok_rows, heads_here, head_width)  13.1 us
    add x15, other arithmetic, add_states(): return earlier + later  12.9 us
    dot_general x4, matrix products, one_block(): jnp.einsum('hqk,khd->qhd', weights, value_block, preferred_element_type=j...  8.58 us
  transfers between devices with their start and end apart: 3, of which 3 were waited for; matrix products, arithmetic and copies ran while one was open for 10% of the time, Pallas kernels for 0%

profile of v1, /device:TPU:31, one launch (start us, length us, event | category | flops | bytes accessed | tf_op | source)
XLA Modules:
  0.0 371.6 jit_solution(486657727391249804)
XLA Ops:
  6.5 2.2 fusion.41
  8.8 1.1 slice_bitcast_fusion.2
  9.9 0.8 pad_maximum_fusion.2
  10.7 4.3 %collective-permute-start = (bf16[2,1024,1,128]{3,1,2,0:T(8,128)(2,1)}, bf16[2,1024,1,128]{3,1,2,0:T(8,128)(2,1)}, u32[]{:S(2)}, u32[]{:S(2)}) collective-permute-start(bf16[2,1024,1,128]{3,1,2,0:T(8,128)(2,1)} %pad_maximum_fusion.2), channel_id=1, source_target_pairs={{0,16},{16,32},{32,48},{48,64},{64,80},{80,96},{96,112},{112,128},... | collective-permute-start | bytes 1572872 | tf_op jit(solution)/shard_map/ppermute | solution.py:22
  16.9 1.8 fusion.16
  18.7 0.7 fusion.30
  19.4 0.9 slice.24
  20.4 2.9 fusion.26
  23.3 2.6 collective-permute-done
  26.0 1.1 slice_bitcast_fusion
  27.1 0.9 pad_maximum_fusion
  28.0 37.0 %while.22 = (s32[]{:T(128)}, f32[4,512,1,128]{1,3,2,0:T(8,128)}, s32[4]{0:T(128)S(1)}, bf16[3072,1,128]{2,0,1:T(8,128)(2,1)}, s32[]{:T(128)}, /*index=5*/bf16[20...) while((s32[]{:T(128)}, f32[4,512,1,128]{1,3,2,0:T(8,128)}, ...), condition=%wide.region_2.3_spmd, body=%wide.region_0.2_spmd.sunk | while | flops 413671424 | bytes 10661624 | solution.py:75
  33.9 1.2 fusion.57
  35.1 2.1 fusion.58
  41.8 0.7 iota_add_fusion.4
  43.1 1.2 fusion.57
  44.4 2.1 fusion.58
  51.0 0.7 iota_add_fusion.4
  52.4 1.2 fusion.57
  53.6 2.1 fusion.58
  60.2 0.7 iota_add_fusion.4
  61.6 1.2 fusion.57
  62.8 2.2 fusion.58
  65.0 1.5 copy.11
  66.6 1.4 multiply_reduce_fusion
  67.9 23.3 %all-gather.3.cloned.1.call-done = f32[4096,128]{1,0:T(8,128)} async-done(((f32[128,128]{1,0:T(8,128)}), f32[4096,128]{1,0:T(8,128)}) %all-gather.3.cloned.1.call-update) | async-done | bytes 2097168 | tf_op jit(solution)/shard_map/all_gather | solution.py:27
  91.3 13.2 %while.23 = (s32[]{:T(128)}, f32[1,128,128]{2,1,0:T(8,128)S(1)}, s32[]{:T(128)}, f32[32,1,128,128]{3,2,1,0:T(8,128)}, s32[]{:T(128)}, /*index=5*/s32[]{:T(128)}, s32[]{:T(128)}) while((s32[]{:T(128)}, f32[1,128,128]{2,1,0:T(8,128)S(1)}, s32[]{:T(128)}, f32[32,1,128,128]{3,2,1,0:T(8,128)}, s32[]{:T(128)}, /*index=5*/s32[]{:T(128)}, ...), condition=%wide.region_6.7_spmd, body=%wide.region_5.6_spmd.sunk | while | flops 16389 | bytes 196731 | solution.py:33
  91.3 0.9 bitcast_add_fusion.2
  92.2 0.9 bitcast_add_fusion.2
  93.0 0.9 bitcast_add_fusion.2
  93.9 0.9 bitcast_add_fusion.2
  94.8 0.9 bitcast_add_fusion.2
  95.7 0.9 bitcast_add_fusion.2
  96.6 0.9 bitcast_add_fusion.2
  97.4 0.9 bitcast_add_fusion.2
  98.3 0.9 bitcast_add_fusion.2
  99.2 0.9 bitcast_add_fusion.2
  100.1 0.9 bitcast_add_fusion.2
  101.0 0.9 bitcast_add_fusion.2
  101.8 0.9 bitcast_add_fusion.2
  102.7 0.9 bitcast_add_fusion.2
  103.6 0.9 bitcast_add_fusion.2
  104.8 1.8 fusion.29
  107.3 30.1 %all_to_all.21 = bf16[16,128,128]{2,1,0:T(8,128)(2,1)S(1)} all-to-all(bf16[16,128,128]{2,1,0:T(8,128)(2,1)S(1)} %multiply_convert_fusion), channel_id=1, replica_groups=mesh['seq'=32,'head'=16] {'head'}, dimensions={0} | all-to-all | bytes 1048576 | tf_op jit(solution)/shard_map/all_to_all | solution.py:131
  137.5 4.3 %stack.11 = bf16[32,64,2048]{2,1,0:T(8,128)(2,1)} broadcast(bf16[64,2048]{1,0:T(8,128)(2,1)S(1)} %copy-done.5), dimensions={1,2} | broadcast | bytes 8650752 | tf_op jit(solution)/shard_map/stack | solution.py:14
  141.7 19.5 %all-to-all-start.1 = ((bf16[32,64,2048]{2,1,0:T(8,128)(2,1)}), bf16[32,64,2048]{2,1,0:T(8,128)(2,1)}, u32[]{:S(2)}, u32[]{:S(2)}) async-start(bf16[32,64,2048]{2,1,0:T(8,128)(2,1)} %stack.11), calls=%async_computation.1 | async-start | bytes 16777216 | tf_op jit(solution)/shard_map/all_to_all | solution.py:15
  161.5 197.8 %all-to-all-done.1 = bf16[32,64,2048]{2,1,0:T(8,128)(2,1)} async-done(((bf16[32,64,2048]{2,1,0:T(8,128)(2,1)}), bf16[32,64,2048]{2,1,0:T(8,128)(2,1)}, u32[]{:S(2)}, u32[]{:S(2)}) %all-to-all-start.1) | async-done | bytes 8388640 | tf_op jit(solution)/shard_map/all_to_all | solution.py:15
  359.3 5.5 %convolution_convert_fusion = bf16[128,2048]{1,0:T(8,128)(2,1)} fusion(bf16[128,2048]{0,1:T(8,128)(2,1)S(1)} %bitcast.117, bf16[2048,2048]{1,0:T(8,128)(2,1)} %bitcast.35), kind=kOutput, calls=%fused_computation.24 | convolution fusion | flops 1074003968 | bytes 9437184 | tf_op jit(solution)/shard_map/dot_general | solution.py:132
  (48 shorter events, 11.5 us)
Async XLA Ops:
  6.5 8.6 %copy-start.1 = (bf16[2048,128]{1,0:T(8,128)(2,1)S(1)}, bf16[2048,128]{1,0:T(8,128)(2,1)}, u32[]{:S(2)}) copy-start(bf16[2048,128]{1,0:T(8,128)(2,1)} %param.9) | copy-start | bytes 1572868
  6.5 8.6 %copy-start.2 = (bf16[2048,128]{1,0:T(8,128)(2,1)S(1)}, bf16[2048,128]{1,0:T(8,128)(2,1)}, u32[]{:S(2)}) copy-start(bf16[2048,128]{1,0:T(8,128)(2,1)} %param.8) | copy-start | bytes 1572868
  6.5 84.7 %all-gather.3.cloned.1.call-start = ((), (), s32[]{:S(2)}) async-start(), calls=%async_computation.2 | async-start | bytes 2162688 | tf_op jit(solution)/shard_map/all_gather | solution.py:27
  10.7 15.2 %collective-permute-start = (bf16[2,1024,1,128]{3,1,2,0:T(8,128)(2,1)}, bf16[2,1024,1,128]{3,1,2,0:T(8,128)(2,1)}, u32[]{:S(2)}, u32[]{:S(2)}) collective-permute-start(bf16[2,1024,1,128]{3,1,2,0:T(8,128)(2,1)} %pad_maximum_fusion.2), channel_id=1, source_target_pairs={{0,16},{16,32},{32,48},{48,64},{64,80},{80,96},{96,112},{112,128},... | collective-permute-start | bytes 1572872 | tf_op jit(solution)/shard_map/ppermute | solution.py:22
  15.9 1.0 copy-start
  23.3 4.7 %copy-start.3 = (bf16[2048,128]{1,0:T(8,128)(2,1)S(1)}, bf16[2048,128]{1,0:T(8,128)(2,1)}, u32[]{:S(2)}) copy-start(bf16[2048,128]{1,0:T(8,128)(2,1)} %param.8) | copy-start | bytes 1572868
  32.5 2.6 copy-start.4
  41.7 2.6 copy-start.4
  51.0 2.6 copy-start.4
  60.2 2.6 copy-start.4
  104.8 32.7 %copy-start.5 = (bf16[64,2048]{1,0:T(8,128)(2,1)S(1)}, bf16[64,2048]{1,0:T(8,128)(2,1)}, u32[]{:S(2)}) copy-start(bf16[64,2048]{1,0:T(8,128)(2,1)} %param.11) | copy-start | bytes 786436
  141.7 217.6 %all-to-all-start.1 = ((bf16[32,64,2048]{2,1,0:T(8,128)(2,1)}), bf16[32,64,2048]{2,1,0:T(8,128)(2,1)}, u32[]{:S(2)}, u32[]{:S(2)}) async-start(bf16[32,64,2048]{2,1,0:T(8,128)(2,1)} %stack.11), calls=%async_computation.1 | async-start | bytes 16777216 | tf_op jit(solution)/shard_map/all_to_all | solution.py:15
Sparse Core Ops, SparseCore 0:
  10.5 80.7 all-gather.2
